TPU v7x, 256 devices: a whole 4x4x8 slice. The times are simulated.
256 devices in a mesh: orb: 8 (over y, core), aux: 32 (over x, z).
Axes of the slice: x: 4, y: 4, z: 8, core: 2. Of those that a mesh axis runs over, the one named last changes fastest.
Arguments:
- factors: bfloat16 [384, 128, 2048], P('orb', None, 'aux'), may hold values from -6 to 6
- amplitudes: bfloat16 [384, 12, 128, 128], P('orb'), may hold values from -0.15625 to 0.15625
- partners: int32 [384, 12], P('orb'), may hold values from 0 to 383, as said below
- metric_tiles: bfloat16 [128, 128, 128], P('aux'), may hold values from -0.1875 to 0.1875
- tile_pos: int32 [128, 2], P('aux'), may hold values from 0 to 15, as said below
Outputs:
- density: bfloat16 [384, 128, 2048], P('orb', 'aux')
Inputs may be any that keep to these rules, and one draw needn't show every extreme that they name: partners[i, 0] = i for every orbital i; the other partners of an orbital are any orbitals, repeats allowed. `tile_pos`: the listed positions (row block, column block) are all distinct, and each of the 16 diagonal positions is listed.
All inputs are finite; a program needn't handle non-finite values.
Results may differ from a plain program's by a relative error of at most 0.0049.
Values may be sent and summed in bfloat16 or wider, within the bound.
A program may use at most 128 MiB of HBM per device.

v0:
```python
import jax
import jax.numpy as jnp
from jax import lax
from jax.sharding import PartitionSpec as P


def placed_terms(tile_set, positions, block_count):
    levels = jnp.arange(block_count, dtype=jnp.int32)
    row_hits = (positions[:, 0:1] == levels[None, :]).astype(jnp.bfloat16)
    col_hits = (positions[:, 1:2] == levels[None, :]).astype(jnp.bfloat16)
    pair_table = (row_hits[:, :, None] * col_hits[:, None, :]).reshape(
        tile_set.shape[0], block_count * block_count
    )
    flat_tiles = tile_set.reshape(tile_set.shape[0], tile_set.shape[1] * tile_set.shape[2])
    return lax.dot_general(
        pair_table, flat_tiles, (((0,), (0,)), ((), ())), preferred_element_type=jnp.float32
    )


def apply_metric(row_block, placed, block_count, span):
    blocks = placed.astype(jnp.bfloat16).reshape(block_count, block_count, span, span)
    rows_split = row_block.reshape(row_block.shape[0], block_count, span)
    result = jnp.einsum("ars,rcsu->acu", rows_split, blocks, preferred_element_type=jnp.float32)
    return result.reshape(row_block.shape[0], block_count * span)


def shards(factors, amplitudes, partners, metric_tiles, tile_pos):
    group_size, domain, aux_part = factors.shape
    flat_factors = factors.reshape(group_size, domain * aux_part)
    gathered = lax.all_gather(flat_factors, "orb", axis=0, tiled=True)
    picked = jnp.take(gathered, partners.reshape(-1), axis=0)
    picked = picked.reshape(partners.shape[0], partners.shape[1], domain, aux_part)
    gammas = jnp.einsum("ikab,ikbp->iap", amplitudes, picked, preferred_element_type=jnp.float32)
    gammas = gammas.astype(jnp.bfloat16)
    owned_rows = lax.all_to_all(gammas, "aux", split_axis=1, concat_axis=2, tiled=True)
    row_block = owned_rows.reshape(owned_rows.shape[0] * owned_rows.shape[1], owned_rows.shape[2])
    span = metric_tiles.shape[1]
    block_count = row_block.shape[1] // span
    placed = placed_terms(
        lax.all_gather(metric_tiles, "aux", axis=0, tiled=True),
        lax.all_gather(tile_pos, "aux", axis=0, tiled=True),
        block_count,
    )
    result = apply_metric(row_block, placed, block_count, span)
    return result.reshape(owned_rows.shape).astype(jnp.bfloat16)


def solution(mesh):
    in_specs = (
        P("orb", None, "aux"),
        P("orb", None, None, None),
        P("orb", None),
        P("aux", None, None),
        P("aux", None),
    )
    out_specs = P("orb", "aux", None)
    return jax.shard_map(shards, mesh=mesh, in_specs=in_specs, out_specs=out_specs, check_vma=False)
```

profile of v0, /device:TPU:24, one launch (start us, length us, event | category | flops | bytes accessed | tf_op | source)
XLA Modules:
  0.0 204.2 jit_solution(7695285728470506883)
XLA Ops:
  6.5 0.0 all-gather.4.cloned.1.call-start
  6.5 1.8 copy.22
  8.3 2.1 %reshape.111 = bf16[48,8192]{1,0:T(8,128)(2,1)} reshape(bf16[48,128,64]{2,1,0:T(8,128)(2,1)S(1)} %copy.22) | data formatting | bytes 1572864 | tf_op jit(solution)/shard_map/reshape | solution.py:29
  10.4 0.0 all-gather.4.cloned.1.call-update
  10.4 0.0 all-gather.6.cloned.1.call-start
  10.4 0.7 all-gather.6.cloned.1.call-update
  11.2 46.1 %all-gather = s32[32,4,2]{1,2,0:T(2,128)S(1)} all-gather(s32[1,4,2]{1,2,0:T(2,128)} %bitcast.51), channel_id=1, replica_groups=mesh['orb'=8,'aux'=32] {'aux'}, dimensions={0}, use_global_device_ids=true | all-gather | bytes 1056 | tf_op jit(solution)/shard_map/all_gather | solution.py:41
  57.2 0.1 reshape.124
  57.3 0.8 copy.23
  58.1 0.1 reshape.112
  58.2 0.7 compare_and_fusion
  58.9 0.1 copy.21
  59.1 0.0 all-gather.4.cloned.1.call-done
  59.1 24.6 %gather_fusion = bf16[576,8192]{1,0:T(8,128)(2,1)} fusion(bf16[384,8192]{1,0:T(8,128)(2,1)} %all-gather.4.cloned.1.call-done, s32[1024]{0:T(1024)S(1)} %pad_clamp_fusion), kind=kCustom, calls=%fused_computation | custom fusion | bytes 18876672 | tf_op jit(solution)/shard_map/jit(_take)/gather | solution.py:31
  83.7 26.1 %gather.7 = bf16[48,12,128,64]{3,2,1,0:T(8,128)(2,1)} reshape(bf16[576,8192]{1,0:T(8,128)(2,1)} %gather_fusion) | data formatting | bytes 18874368 | tf_op jit(solution)/shard_map/jit(_take)/gather | solution.py:31
  109.9 14.9 %fusion.10 = bf16[48,128,64]{1,2,0:T(8,128)(2,1)S(1)} fusion(bf16[48,12,128,128]{3,2,1,0:T(8,128)(2,1)} %param.6, bf16[48,12,128,64]{3,2,1,0:T(8,128)(2,1)} %gather.7, pred[48,12]{1,0:T(8,128)(4,1)S(1)} %copy.21), kind=kOutput, calls=%fused_computation.13 | convolution fusion | flops 1213071360 | bytes 29098560 | tf_op jit(solution)/shard_map/ikab,ikbp->iap/dot_general | solution.py:33
  124.7 1.0 copy.25
  125.7 1.9 reshape.129
  127.6 6.6 %all-to-all-start = ((bf16[32,2,6144]{2,1,0:T(2,128)(2,1)}), bf16[32,2,6144]{2,1,0:T(2,128)(2,1)S(1)}, u32[]{:S(2)}, u32[]{:S(2)}) async-start(bf16[32,2,6144]{2,1,0:T(2,128)(2,1)} %reshape.129), calls=%async_computation | async-start | bytes 1572864 | tf_op jit(solution)/shard_map/all_to_all | solution.py:35
  134.2 11.8 %all-gather.6.cloned.1.call-done = bf16[128,128,128]{2,1,0:T(8,128)(2,1)} async-done(((bf16[4,128,128]{2,1,0:T(8,128)(2,1)}), bf16[128,128,128]{2,1,0:T(8,128)(2,1)}) %all-gather.6.cloned.1.call-update) | async-done | bytes 4194320 | tf_op jit(solution)/shard_map/all_gather | solution.py:40
  146.1 8.8 %fusion.4 = bf16[32,8,128,128]{3,1,2,0:T(8,128)(2,1)} fusion(bf16[128,256]{0,1:T(8,128)(2,1)S(1)} %bitcast.50, bf16[16,8,128,128]{3,2,1,0:T(8,128)(2,1)} %bitcast.49), kind=kOutput, calls=%fused_computation.7 | convolution fusion | flops 1077936128 | bytes 12648448 | tf_op jit(solution)/shard_map/dot_general | solution.py:15
  154.9 9.2 %copy.35 = bf16[32,8,128,128]{3,2,1,0:T(8,128)(2,1)} copy(bf16[32,8,128,128]{3,1,2,0:T(8,128)(2,1)} %fusion.4) | data formatting | bytes 16777216
  164.1 10.4 %bitcast_bitcast_fusion = bf16[16,128,16,128]{1,3,0,2:T(8,128)(2,1)} fusion(bf16[16,16,128,128]{3,2,1,0:T(8,128)(2,1)} %bitcast.45), kind=kLoop, calls=%fused_computation.6 | loop fusion | bytes 16777216 | tf_op jit(solution)/shard_map/ars,rcsu->acu/dot_general | solution.py:23
  174.4 12.3 %copy.28 = bf16[16,128,16,128]{3,1,0,2:T(8,128)(2,1)} copy(bf16[16,128,16,128]{1,3,0,2:T(8,128)(2,1)} %bitcast_bitcast_fusion) | data formatting | bytes 16777216 | tf_op jit(solution)/shard_map/ars,rcsu->acu/dot_general | solution.py:23
  186.7 0.0 all-to-all-done
  186.8 1.0 reshape.130
  187.8 1.0 copy.26
  188.8 0.7 dot_general.16
  189.5 6.3 %fusion.7 = bf16[48,4,2048]{2,0,1:T(8,128)(2,1)S(1)} fusion(bf16[2048,16,128,1]{2,0,1,3:T(8,128)(2,1)} %bitcast.46, bf16[48,4,16,128]{3,2,1,0:T(8,128)(2,1)S(1)} %dot_general.16), kind=kOutput, calls=%fused_computation.11 | convolution fusion | flops 1611005952 | bytes 9961472 | tf_op jit(solution)/shard_map/ars,rcsu->acu/dot_general | solution.py:23
  195.9 1.5 copy.30
  (6 shorter events, 0.0 us)
Async XLA Ops:
  6.5 52.6 %all-gather.4.cloned.1.call-start = ((), (), s32[]{:S(2)}) async-start(), calls=%async_computation.1 | async-start | bytes 7077888 | tf_op jit(solution)/shard_map/all_gather | solution.py:30
  10.4 135.7 %all-gather.6.cloned.1.call-start = ((), (), s32[]{:S(2)}) async-start(), calls=%async_computation.2 | async-start | bytes 4325376 | tf_op jit(solution)/shard_map/all_gather | solution.py:40
  127.6 59.2 %all-to-all-start = ((bf16[32,2,6144]{2,1,0:T(2,128)(2,1)}), bf16[32,2,6144]{2,1,0:T(2,128)(2,1)S(1)}, u32[]{:S(2)}, u32[]{:S(2)}) async-start(bf16[32,2,6144]{2,1,0:T(2,128)(2,1)} %reshape.129), calls=%async_computation | async-start | bytes 1572864 | tf_op jit(solution)/shard_map/all_to_all | solution.py:35
Sparse Core Ops, SparseCore 0:
  10.5 44.1 all-gather.3
  57.4 88.6 all-gather.5
where the time goes:
time: 206 us; the launch traced here: 204 us
  local copies, waits for them, and re-layouts  94.6 us (46%)
  blocking collectives  46.1 us (22%)
  matrix products  30 us (15%)
  between operations  13.5 us (7%)
  waiting for transfers between devices  12.6 us (6%)
  starting transfers between devices  6.66 us (3%)
    gather x2, local copies, waits for them, and re-layouts, shards(): picked = jnp.take(gathered, partners.reshape(-1), axis=0)  50.7 us
    all_gather x1, blocking collectives, shards(): lax.all_gather(tile_pos, 'aux', axis=0, tiled=True)  46.1 us
    dot_general x3, local copies, waits for them, and re-layouts, apply_metric(): jnp.einsum('ars,rcsu->acu', rows_split, blocks, preferred_element_type=jn...  23.4 us
    dot_general x1, matrix products, shards(): jnp.einsum('ikab,ikbp->iap', amplitudes, picked, preferred_element_type=j...  14.9 us
    unnamed x6, local copies, waits for them, and re-layouts  14.7 us
    all_gather x1, waiting for transfers between devices, shards(): lax.all_gather(metric_tiles, 'aux', axis=0, tiled=True)  11.8 us
    dot_general x1, matrix products, placed_terms(): lax.dot_general(pair_table, flat_tiles, (((0,), (0,)), ((), ())), preferr...  8.82 us
    all_to_all x1, starting transfers between devices, shards(): lax.all_to_all(gammas, 'aux', split_axis=1, concat_axis=2, tiled=True)  6.62 us
  transfers between devices with their start and end apart: 3, of which 1 were waited for; matrix products, arithmetic and copies ran while one was open for 54% of the time, Pallas kernels for 0%

commit v1 on v0

v1 whole, which is shorter than its diff:
```python
import functools

import jax
import jax.numpy as jnp
from jax import lax
from jax.experimental import pallas as pl
from jax.experimental.pallas import tpu as pltpu
from jax.sharding import PartitionSpec as P

MESH = pl.DeviceIdType.MESH
NY, NX, NZ = 4, 4, 8
NAUX = NX * NZ
CHUNKS = 2
PIECES = 4
SUBS = 3
NBLK = 16
XPLUS = (0, 1, 2, 4)
XMINUS = (5, 6, 7, 3)


def kernel(ft, amp, part, tiles, meta, out, *scratch):
    fbuf = scratch[:CHUNKS]
    (ampv, mbuf, stage, sbuf, rbuf, lhs, inv_v, inv_s) = scratch[CHUNKS:CHUNKS + 8]
    (loc, ysend, ssend, yp, ym, y2p, y2m, sib,
     msend, rzp, rzm, rxp, rxm, rx2, msib, asend, arecv) = scratch[CHUNKS + 8:]

    o = lax.axis_index("orb")
    s = lax.axis_index("aux")
    y, h = o // 2, o % 2
    x, z = s // NZ, s % NZ
    own, npair = amp.shape[0], amp.shape[1]
    nt = tiles.shape[0]
    span = tiles.shape[1]
    half = nt // 2
    pw = ft.shape[1] // CHUNKS
    lanes = 128
    per = lanes // pw
    ng = own // per
    gl = ng // SUBS
    npc = own // PIECES
    nrow = ng * 4

    def orb_at(dy):
        return lax.rem(y + dy + NY, NY) * 2 + h

    def aux_at(dx, dz):
        return lax.rem(x + dx + NX, NX) * NZ + lax.rem(z + dz + NZ, NZ)

    sibling = (y * 2 + 1 - h, s)
    yplus, yminus = (orb_at(1), s), (orb_at(-1), s)
    xplus, xminus = (o, aux_at(1, 0)), (o, aux_at(-1, 0))
    zplus, zminus = (o, aux_at(0, 1)), (o, aux_at(0, -1))

    def remote(src, dst, ssem, rsem, dev):
        return pltpu.make_async_remote_copy(
            src_ref=src, dst_ref=dst, send_sem=ssem, recv_sem=rsem, device_id=dev, device_id_type=MESH)

    def recv(ref, ssem, rsem):
        remote(ref, ref, ssem, rsem, sibling).wait_recv()

    def sent(ref, ssem, rsem):
        remote(ref, ref, ssem, rsem, sibling).wait_send()

    mine = pl.ds(s * nt, nt)
    load_tiles = pltpu.make_async_copy(tiles, mbuf.at[mine, pl.ds(0, span)], loc.at[0])
    load_meta = pltpu.make_async_copy(meta, mbuf.at[mine, pl.ds(span, 16)], loc.at[1])
    load_tiles.start()
    load_meta.start()
    load_own = [
        pltpu.make_async_copy(ft.at[:, pl.ds(c * pw, pw), :], fbuf[c].at[pl.ds(o * own, own)], loc.at[2 + c])
        for c in range(CHUNKS)
    ]
    for copy in load_own:
        copy.start()
    load_amp = pltpu.make_async_copy(amp, ampv, loc.at[2 + CHUNKS])
    load_amp.start()

    barrier = pltpu.get_barrier_semaphore()
    for dev in (sibling, yplus, yminus, xplus, xminus, zplus, zminus):
        pl.semaphore_signal(barrier, inc=1, device_id=dev, device_id_type=MESH)
    pl.semaphore_wait(barrier, 7)

    def fpiece(c, orb, q):
        return fbuf[c].at[pl.ds(orb * own + q * npc, npc)]

    def to_sibling(c, ref):
        remote(ref, ref, ssend.at[c], sib.at[c], sibling).start()

    def gather_start(c):
        for q in range(PIECES):
            src = ft.at[pl.ds(q * npc, npc), pl.ds(c * pw, pw), :]
            dst = fpiece(c, o, q)
            remote(src, dst, ysend.at[c], yp.at[c, q], yplus).start()
            remote(src, dst, ysend.at[c], ym.at[c, q], yminus).start()
        for q in range(PIECES):
            src = ft.at[pl.ds(q * npc, npc), pl.ds(c * pw, pw), :]
            remote(src, fpiece(c, o, q), ssend.at[c], sib.at[c], sibling).start()

    def gather_round(c, q):
        below, above = fpiece(c, orb_at(-1), q), fpiece(c, orb_at(1), q)
        recv(below, ysend.at[c], yp.at[c, q])
        if q < PIECES // 2:
            remote(below, below, ysend.at[c], y2p.at[c, q], yplus).start()
        to_sibling(c, below)
        recv(above, ysend.at[c], ym.at[c, q])
        if q >= PIECES // 2:
            remote(above, above, ysend.at[c], y2m.at[c, q - PIECES // 2], yminus).start()
        to_sibling(c, above)

    def gather_far(c, q):
        far = fpiece(c, orb_at(2), q)
        if q < PIECES // 2:
            recv(far, ysend.at[c], y2p.at[c, q])
        else:
            recv(far, ysend.at[c], y2m.at[c, q - PIECES // 2])
        to_sibling(c, far)

    def gather_done(c):
        recv(fbuf[c].at[pl.ds(0, NY * own)], ssend.at[c], sib.at[c])
        load_own[c].wait()

    def shard(dx, idx):
        dz = -idx if idx <= NZ // 2 else idx - NZ // 2
        return mbuf.at[pl.ds(aux_at(dx, dz) * nt + h * half, half)]

    def tiles_out(idx):
        ref = shard(0, idx)
        if idx < NZ // 2:
            remote(ref, ref, msend.at[0], rzp.at[idx], zplus).start()
        if idx == 0:
            remote(ref, ref, msend.at[0], rzm.at[0], zminus).start()
        elif idx > NZ // 2 and idx < NZ - 1:
            remote(ref, ref, msend.at[0], rzm.at[idx - NZ // 2], zminus).start()
        remote(ref, ref, msend.at[1], rxp.at[idx], xplus).start()
        remote(ref, ref, msend.at[2], rxm.at[idx], xminus).start()
        if idx:
            remote(ref, ref, msend.at[3], msib.at[0], sibling).start()

    def tiles_x(idx):
        left, right = shard(-1, idx), shard(1, idx)
        recv(left, msend.at[1], rxp.at[idx])
        if idx in XPLUS:
            remote(left, left, msend.at[4], rx2.at[idx], xplus).start()
        remote(left, left, msend.at[3], msib.at[0], sibling).start()
        recv(right, msend.at[2], rxm.at[idx])
        if idx in XMINUS:
            remote(right, right, msend.at[4], rx2.at[idx], xminus).start()
        remote(right, right, msend.at[3], msib.at[0], sibling).start()

    def tiles_round(k):
        if k <= NZ // 2:
            recv(shard(0, k), msend.at[0], rzp.at[k - 1])
            tiles_out(k)
        if k < NZ // 2:
            recv(shard(0, NZ // 2 + k), msend.at[0], rzm.at[k - 1])
            tiles_out(NZ // 2 + k)
        tiles_x(k - 1)
        if k >= 2 and k - 1 < NZ // 2:
            tiles_x(NZ // 2 + k - 1)

    def tiles_far():
        for idx in range(NZ):
            far = shard(2, idx)
            recv(far, msend.at[4], rx2.at[idx])
            remote(far, far, msend.at[3], msib.at[0], sibling).start()
        recv(mbuf.at[pl.ds(0, (NAUX - 1) * half)], msend.at[3], msib.at[0])

    def contract(c, g):
        blank = {n: jnp.zeros((n * pw, lanes), jnp.bfloat16) for n in range(1, per)}
        left, right = [], []
        for k in range(npair):
            for q in range(per):
                i = q * ng + g
                left.append(ampv[i, k])
                rows = [fbuf[c][part[k, i]]]
                if q:
                    rows.insert(0, blank[q])
                if q < per - 1:
                    rows.append(blank[per - 1 - q])
                right.append(jnp.concatenate(rows, axis=0))
        return lax.dot_general(
            jnp.concatenate(left, axis=1), jnp.concatenate(right, axis=1),
            (((1,), (1,)), ((), ())), preferred_element_type=jnp.float32)

    def contract_sub(c, u):
        def body(g, carry):
            value = contract(c, u * gl + g)
            at = pl.multiple_of(g * 4, 4)
            for r in range(NAUX):
                stage[r, pl.ds(at, 4), :] = value[4 * r:4 * r + 4, :]
            return carry
        lax.fori_loop(0, gl, body, 0)
        rows = pl.ds(u * gl * 4, gl * 4)

        def pack(r, carry):
            sbuf[c, r, rows, :] = stage[r].astype(jnp.bfloat16)
            return carry
        lax.fori_loop(0, NAUX, pack, 0)

        def send(d, carry):
            to = lax.rem(s + d, NAUX)
            remote(sbuf.at[c, to, rows], rbuf.at[c, s, rows], asend.at[c, u], arecv.at[c, u], (o, to)).start()
            return carry
        lax.fori_loop(1, NAUX, send, 0)
        rbuf[c, s, rows, :] = sbuf[c, s, rows, :]

    load_tiles.wait()
    load_meta.wait()
    mbuf[NAUX * nt] = jnp.zeros(mbuf.shape[1:], jnp.bfloat16)
    gather_start(0)
    tiles_out(0)
    for q in range(PIECES):
        gather_round(0, q)
        tiles_round(q + 1)
    for c in range(1, CHUNKS):
        gather_start(c)
    for q in range(PIECES):
        gather_far(0, q)
    tiles_x(NZ // 2)
    tiles_far()
    gather_done(0)
    load_amp.wait()
    for c in range(CHUNKS):
        for u in range(SUBS):
            contract_sub(c, u)
            if c + 1 < CHUNKS:
                for q in range(PIECES):
                    if q * SUBS // PIECES == u:
                        gather_round(c + 1, q)
        if c + 1 < CHUNKS:
            for q in range(PIECES):
                gather_far(c + 1, q)
            gather_done(c + 1)

    def look(t, carry):
        low, high = carry
        key = mbuf[t, pl.ds(span, 16), :].astype(jnp.int32)
        lane = lax.broadcasted_iota(jnp.int32, key.shape, 1)
        return jnp.where(key == lane, t, low), jnp.where(key == lane + lanes, t, high)

    none = jnp.full((16, lanes), NAUX * nt, jnp.int32)
    low, high = lax.fori_loop(0, NAUX * nt, look, (none, none))
    inv_v[0] = low[0:8]
    inv_v[1] = high[0:8]
    copy = pltpu.make_async_copy(inv_v, inv_s, loc.at[3 + CHUNKS])
    copy.start()
    copy.wait()

    for c in range(CHUNKS):
        for u in range(SUBS):
            ref = rbuf.at[c, pl.ds(0, NAUX - 1), pl.ds(u * gl * 4, gl * 4)]
            recv(ref, asend.at[c, u], arecv.at[c, u])

    def arrange(b, carry):
        blocks = [rbuf[c, 2 * b + e] for e in range(2) for c in range(CHUNKS)]
        at = pl.multiple_of(b * lanes, lanes)
        for q in range(per):
            lhs[pl.ds(q * nrow, nrow), pl.ds(at, lanes)] = jnp.concatenate(
                [blk[:, q * pw:(q + 1) * pw] for blk in blocks], axis=1)
        return carry
    lax.fori_loop(0, NBLK, arrange, 0)

    def columns(cb, carry):
        rows = []
        for r in range(NBLK):
            pair = []
            for e in range(2):
                at = r * NBLK + 2 * cb + e
                pair.append(mbuf[inv_s[at // lanes, 0, lax.rem(at, lanes)], pl.ds(0, span), :])
            rows.append(jnp.concatenate(pair, axis=1))
        value = jnp.dot(lhs[...], jnp.concatenate(rows, axis=0), preferred_element_type=jnp.float32)
        out[:, pl.ds(pl.multiple_of(cb * 2 * lanes, 2 * lanes), 2 * lanes)] = value.astype(jnp.bfloat16)
        return carry
    lax.fori_loop(0, NBLK // 2, columns, 0)

    for c in range(CHUNKS):
        sent(fbuf[c].at[pl.ds(0, 3 * own)], ysend.at[c], yp.at[c, 0])
        sent(fbuf[c].at[pl.ds(0, NY * own)], ssend.at[c], sib.at[c])
        for u in range(SUBS):
            ref = sbuf.at[c, pl.ds(0, NAUX - 1), pl.ds(u * gl * 4, gl * 4)]
            sent(ref, asend.at[c, u], arecv.at[c, u])
    sent(mbuf.at[pl.ds(0, (NZ - 1) * half)], msend.at[0], msib.at[0])
    sent(mbuf.at[pl.ds(0, NZ * half)], msend.at[1], msib.at[0])
    sent(mbuf.at[pl.ds(0, NZ * half)], msend.at[2], msib.at[0])
    sent(mbuf.at[pl.ds(0, (NAUX - 1) * half)], msend.at[3], msib.at[0])
    sent(mbuf.at[pl.ds(0, NZ * half)], msend.at[4], msib.at[0])


def shards(factors, amplitudes, partners, metric_tiles, tile_pos):
    own, domain, aux_part = factors.shape
    npair = partners.shape[1]
    nt, span = metric_tiles.shape[0], metric_tiles.shape[1]
    norb = own * 2 * NY
    pw = aux_part // CHUNKS
    ng = own * pw // 128
    keys = (tile_pos[:, 0] * NBLK + tile_pos[:, 1]).astype(jnp.bfloat16)
    meta = jnp.broadcast_to(keys[:, None, None], (nt, 16, 128))
    dma = pltpu.SemaphoreType.DMA
    anywhere = pl.BlockSpec(memory_space=pl.ANY)
    rows = own * domain // NAUX
    result = pl.pallas_call(
        kernel,
        out_shape=jax.ShapeDtypeStruct((rows, aux_part * NAUX), jnp.bfloat16),
        in_specs=[anywhere, anywhere, pl.BlockSpec(memory_space=pltpu.SMEM), anywhere, anywhere],
        out_specs=pl.BlockSpec(memory_space=pltpu.VMEM),
        scratch_shapes=[pltpu.VMEM((norb, pw, domain), jnp.bfloat16)] * CHUNKS + [
            pltpu.VMEM(amplitudes.shape, jnp.bfloat16),
            pltpu.VMEM((NAUX * nt + 1, span + 16, span), jnp.bfloat16),
            pltpu.VMEM((NAUX, 4 * ng // SUBS, 128), jnp.float32),
            pltpu.VMEM((CHUNKS, NAUX, 4 * ng, 128), jnp.bfloat16),
            pltpu.VMEM((CHUNKS, NAUX, 4 * ng, 128), jnp.bfloat16),
            pltpu.VMEM((rows, aux_part * NAUX), jnp.bfloat16),
            pltpu.VMEM((2, 8, 128), jnp.int32),
            pltpu.SMEM((2, 8, 128), jnp.int32),
            dma((4 + CHUNKS,)),
            dma((CHUNKS,)),
            dma((CHUNKS,)),
            dma((CHUNKS, PIECES)),
            dma((CHUNKS, PIECES)),
            dma((CHUNKS, PIECES // 2)),
            dma((CHUNKS, PIECES // 2)),
            dma((CHUNKS,)),
            dma((5,)),
            dma((NZ // 2,)),
            dma((NZ // 2,)),
            dma((NZ,)),
            dma((NZ,)),
            dma((NZ,)),
            dma((1,)),
            dma((CHUNKS, SUBS)),
            dma((CHUNKS, SUBS)),
        ],
        compiler_params=pltpu.CompilerParams(
            collective_id=0, has_side_effects=True, vmem_limit_bytes=60 * 1024 * 1024),
    )(jnp.swapaxes(factors, 1, 2), amplitudes, partners.T, metric_tiles, meta)
    return result.reshape(own, rows // own, aux_part * NAUX)


def solution(mesh):
    in_specs = (
        P("orb", None, "aux"),
        P("orb", None, None, None),
        P("orb", None),
        P("aux", None, None),
        P("aux", None),
    )
    out_specs = P("orb", "aux", None)
    return jax.shard_map(shards, mesh=mesh, in_specs=in_specs, out_specs=out_specs, check_vma=False)
```

time: 206 us -> 73.9 us (0.36)
  the two profiles are of different devices: /device:TPU:24 before, /device:TPU:1 now
where the time goes in v1:
time: 73.9 us; the launch traced here: 73.7 us
  Pallas kernels  69.9 us (95%)
  local copies, waits for them, and re-layouts  3.06 us (4%)
  other arithmetic  0.76 us (1%)
    pallas_call x1, Pallas kernels, shards(): pl.pallas_call(kernel, out_shape=jax.ShapeDtypeStruct((rows, aux_part * N...  69.9 us
    reshape x1, local copies, waits for them, and re-layouts, shards(): return result.reshape(own, rows // own, aux_part * NAUX)  2.38 us

profile of v1, /device:TPU:1, one launch (start us, length us, event | category | flops | bytes accessed | tf_op | source)
XLA Modules:
  0.0 73.7 jit_solution(12676539085049470986)
XLA Ops:
  0.0 0.8 %convert_bitcast_fusion = bf16[4]{0:T(256)(128)(2,1)S(1)} fusion(s32[4,2]{0,1:T(2,128)} %param.9), kind=kLoop, calls=%fused_computation | loop fusion | flops 12 | bytes 40 | tf_op jit(solution)/shard_map/convert_element_type | solution.py:296
  0.8 0.7 broadcast_in_dim.2.meta
  1.4 69.9 %shard_map.55 = bf16[192,2048]{1,0:T(8,128)(2,1)} custom-call(bf16[48,64,128]{2,1,0:T(8,128)(2,1)} %bitcast.4, bf16[48,12,128,128]{3,2,1,0:T(8,128)(2,1)} %amp.1, s32[12,48]{1,0:T(8,128)} %bitcast.5, bf16[4,128,128]{2,1,0:T(8,128)(2,1)} %tiles.1, bf16[4,16,128]{2,1,0:T(8,128)(2,1)} %broadcast_in_dim.2.meta), custom_call_target="tpu_custom_call" | custom-call | tf_op jit(solution)/shard_map/pallas_call | solution.py:301
  71.3 2.4 %reshape.18 = bf16[48,4,2048]{2,1,0:T(4,128)(2,1)} reshape(bf16[192,2048]{1,0:T(8,128)(2,1)} %shard_map.55) | data formatting | bytes 1572864 | tf_op jit(solution)/shard_map/reshape | solution.py:336

commit v2 on v1

v2 whole, which is shorter than its diff:
```python
import jax
import jax.numpy as jnp
from jax import lax
from jax.experimental import pallas as pl
from jax.experimental.pallas import tpu as pltpu
from jax.sharding import PartitionSpec as P

MESH = pl.DeviceIdType.MESH
NY, NX, NZ = 4, 4, 8
NAUX = NX * NZ
WIDTHS = (32, 32)
STARTS = (0, 32)
CHUNKS = len(WIDTHS)
PIECES = (4, 4)
SUBS = 3
NBLK = 16
LANES = 128
WAVES = NZ // 2 - 1
XPLUS = (0, 1, 2, 4)
XMINUS = (5, 6, 7, 3)


def kernel(ft, amp, part, tiles, pos, out, *scratch):
    fbuf, sbuf, rbuf, lhs = (scratch[n * CHUNKS:(n + 1) * CHUNKS] for n in range(4))
    (ampv, mbuf, stage, acc, inv_v, inv_s) = scratch[4 * CHUNKS:4 * CHUNKS + 6]
    (loc, ysend, ssend, yp, ym, y2p, y2m, sib,
     msend, rzp, rzm, rxp, rxm, rx2, msib, asend, arecv, wave) = scratch[4 * CHUNKS + 6:]

    o = lax.axis_index("orb")
    s = lax.axis_index("aux")
    y, h = o // 2, o % 2
    x, z = s // NZ, s % NZ
    own, npair = amp.shape[0], amp.shape[1]
    nt, span = tiles.shape[0], tiles.shape[1]
    half = nt // 2
    pers = [LANES // pw for pw in WIDTHS]
    groups = [own // per for per in pers]

    def orb_at(dy):
        return lax.rem(y + dy + NY, NY) * 2 + h

    def aux_at(dx, dz):
        return lax.rem(x + dx + NX, NX) * NZ + lax.rem(z + dz + NZ, NZ)

    columns_at = [lax.rem(x + dx, NX) * NZ for dx in range(NX)]
    sibling = (y * 2 + 1 - h, s)
    yplus, yminus = (orb_at(1), s), (orb_at(-1), s)
    xplus, xminus = (o, aux_at(1, 0)), (o, aux_at(-1, 0))
    zplus, zminus = (o, aux_at(0, 1)), (o, aux_at(0, -1))

    def remote(src, dst, ssem, rsem, dev):
        return pltpu.make_async_remote_copy(
            src_ref=src, dst_ref=dst, send_sem=ssem, recv_sem=rsem, device_id=dev, device_id_type=MESH)

    def recv(ref, ssem, rsem):
        remote(ref, ref, ssem, rsem, sibling).wait_recv()

    def sent(ref, ssem, rsem):
        remote(ref, ref, ssem, rsem, sibling).wait_send()

    def signal(sem, dev):
        pl.semaphore_signal(sem, inc=1, device_id=dev, device_id_type=MESH)

    barrier = pltpu.get_barrier_semaphore()
    for dev in (sibling, yplus, yminus, xplus, xminus, zplus, zminus):
        signal(barrier, dev)

    mine = pl.ds(s * nt, nt)
    load_tiles = pltpu.make_async_copy(tiles, mbuf.at[mine, pl.ds(0, span)], loc.at[0])
    load_tiles.start()
    for t in range(nt):
        key = (pos[0, t] * NBLK + pos[1, t]).astype(jnp.float32)
        mbuf[s * nt + t, pl.ds(span, 16), :] = jnp.full((16, LANES), key, jnp.float32).astype(jnp.bfloat16)
    mbuf[NAUX * nt] = jnp.zeros(mbuf.shape[1:], jnp.bfloat16)
    load_own = [
        pltpu.make_async_copy(
            ft.at[:, pl.ds(STARTS[c], WIDTHS[c]), :], fbuf[c].at[pl.ds(o * own, own)], loc.at[2 + c])
        for c in range(CHUNKS)
    ]
    load_amp = pltpu.make_async_copy(amp, ampv, loc.at[2 + CHUNKS])

    def fpiece(c, orb, q):
        npc = own // PIECES[c]
        return fbuf[c].at[pl.ds(orb * own + q * npc, npc)]

    def to_sibling(c, ref):
        remote(ref, ref, ssend.at[c], sib.at[c], sibling).start()

    def gather_start(c):
        npc = own // PIECES[c]
        for q in range(PIECES[c]):
            src = ft.at[pl.ds(q * npc, npc), pl.ds(STARTS[c], WIDTHS[c]), :]
            dst = fpiece(c, o, q)
            remote(src, dst, ysend.at[c], yp.at[c, q], yplus).start()
            remote(src, dst, ysend.at[c], ym.at[c, q], yminus).start()
        for q in range(PIECES[c]):
            src = ft.at[pl.ds(q * npc, npc), pl.ds(STARTS[c], WIDTHS[c]), :]
            remote(src, fpiece(c, o, q), ssend.at[c], sib.at[c], sibling).start()

    def gather_round(c, q):
        below, above = fpiece(c, orb_at(-1), q), fpiece(c, orb_at(1), q)
        mid = PIECES[c] // 2
        recv(below, ysend.at[c], yp.at[c, q])
        if q < mid:
            remote(below, below, ysend.at[c], y2p.at[c, q], yplus).start()
        to_sibling(c, below)
        recv(above, ysend.at[c], ym.at[c, q])
        if q >= mid:
            remote(above, above, ysend.at[c], y2m.at[c, q - mid], yminus).start()
        to_sibling(c, above)

    def gather_far(c, q):
        mid = PIECES[c] // 2
        low, high = fpiece(c, orb_at(2), q), fpiece(c, orb_at(2), q + mid)
        recv(low, ysend.at[c], y2p.at[c, q])
        to_sibling(c, low)
        recv(high, ysend.at[c], y2m.at[c, q])
        to_sibling(c, high)

    def gather_done(c):
        recv(fbuf[c].at[pl.ds(0, NY * own)], ssend.at[c], sib.at[c])
        load_own[c].wait()

    def shard(dx, idx):
        dz = -idx if idx <= NZ // 2 else idx - NZ // 2
        return mbuf.at[pl.ds(aux_at(dx, dz) * nt + h * half, half)]

    def tiles_out(idx):
        ref = shard(0, idx)
        if idx < NZ // 2:
            remote(ref, ref, msend.at[0], rzp.at[idx], zplus).start()
        if idx == 0:
            remote(ref, ref, msend.at[0], rzm.at[0], zminus).start()
        elif idx > NZ // 2 and idx < NZ - 1:
            remote(ref, ref, msend.at[0], rzm.at[idx - NZ // 2], zminus).start()
        remote(ref, ref, msend.at[1], rxp.at[idx], xplus).start()
        remote(ref, ref, msend.at[2], rxm.at[idx], xminus).start()
        if idx:
            remote(ref, ref, msend.at[3], msib.at[0], sibling).start()

    def tiles_x(idx):
        left, right = shard(-1, idx), shard(1, idx)
        recv(left, msend.at[1], rxp.at[idx])
        if idx in XPLUS:
            remote(left, left, msend.at[4], rx2.at[idx], xplus).start()
        remote(left, left, msend.at[3], msib.at[0], sibling).start()
        recv(right, msend.at[2], rxm.at[idx])
        if idx in XMINUS:
            remote(right, right, msend.at[4], rx2.at[idx], xminus).start()
        remote(right, right, msend.at[3], msib.at[0], sibling).start()

    def tiles_z(k):
        recv(shard(0, k), msend.at[0], rzp.at[k - 1])
        tiles_out(k)
        if k < NZ // 2:
            recv(shard(0, NZ // 2 + k), msend.at[0], rzm.at[k - 1])
            tiles_out(NZ // 2 + k)

    def tiles_far(idx):
        far = shard(2, idx)
        recv(far, msend.at[4], rx2.at[idx])
        remote(far, far, msend.at[3], msib.at[0], sibling).start()

    def tiles_done():
        recv(mbuf.at[pl.ds(0, (NAUX - 1) * half)], msend.at[3], msib.at[0])

    def wave_out(k):
        for dev in (zplus, zminus) if k < WAVES else (xplus, xminus):
            signal(wave.at[k], dev)

    def wave_next(k):
        pl.semaphore_wait(wave.at[k], 2)
        if k < WAVES + 1:
            wave_out(k + 1)

    def contract(c, g):
        pw, per, ng = WIDTHS[c], pers[c], groups[c]
        blank = {n: jnp.zeros((n * pw, LANES), jnp.bfloat16) for n in range(1, per)}
        left, right = [], []
        for k in range(npair):
            for q in range(per):
                i = q * ng + g
                left.append(ampv[i, k])
                rows = [fbuf[c][part[k, i]]]
                if q:
                    rows.insert(0, blank[q])
                if q < per - 1:
                    rows.append(blank[per - 1 - q])
                right.append(jnp.concatenate(rows, axis=0))
        return lax.dot_general(
            jnp.concatenate(left, axis=1), jnp.concatenate(right, axis=1),
            (((1,), (1,)), ((), ())), preferred_element_type=jnp.float32)

    def contract_part(c, u, events=()):
        gl = groups[c] // SUBS
        rows = pl.ds(0, gl * 4)
        for g in range(gl):
            value = contract(c, u * gl + g)
            for r in range(NAUX):
                stage[r, g * 4:g * 4 + 4, :] = value[4 * r:4 * r + 4, :]
            for event in events[g:g + 1]:
                event()

        def pack(r, carry):
            sbuf[c][u, r] = stage[r, rows, :].astype(jnp.bfloat16)
            return carry
        lax.fori_loop(0, NAUX, pack, 0, unroll=4)

        def put(to):
            remote(sbuf[c].at[u, to], rbuf[c].at[u, s], asend.at[c, u], arecv.at[c, u], (o, to)).start()

        def send(a, carry):
            dz = NZ // 2 + (1 - 2 * (a % 2)) * ((a + 1) // 2)
            there = lax.rem(z + dz, NZ)
            for dx in (2, 1, 3, 0):
                put(columns_at[dx] + there)
            return carry
        lax.fori_loop(0, NZ - 1, send, 0)
        for dx in (2, 1, 3):
            put(columns_at[dx] + z)
        rbuf[c][u, s] = sbuf[c][u, s]

    def look_up():
        def look(t, carry):
            low, high = carry
            key = mbuf[t, pl.ds(span, 16), :].astype(jnp.int32)
            lane = lax.broadcasted_iota(jnp.int32, key.shape, 1)
            return jnp.where(key == lane, t, low), jnp.where(key == lane + LANES, t, high)

        none = jnp.full((16, LANES), NAUX * nt, jnp.int32)
        low, high = lax.fori_loop(0, NAUX * nt, look, (none, none), unroll=8)
        inv_v[0] = low[0:8]
        inv_v[1] = high[0:8]
        copy = pltpu.make_async_copy(inv_v, inv_s, loc.at[1])
        copy.start()
        copy.wait()

    def arrange(c, u):
        pw, per, ng = WIDTHS[c], pers[c], groups[c]
        rows = 4 * ng // SUBS
        recv(rbuf[c].at[u, pl.ds(0, NAUX - 1)], asend.at[c, u], arecv.at[c, u])

        def body(b, carry):
            at = pl.multiple_of(b * LANES, LANES)
            blocks = [rbuf[c][u, b * per + e] for e in range(per)]
            for q in range(per):
                lhs[c][pl.ds((q * SUBS + u) * rows, rows), pl.ds(at, LANES)] = jnp.concatenate(
                    [blk[:, q * pw:(q + 1) * pw] for blk in blocks], axis=1)
            return carry
        lax.fori_loop(0, NAUX // per, body, 0, unroll=2)

    def product(cs, first, last):
        def columns(cb, carry):
            at = pl.ds(pl.multiple_of(cb * 2 * LANES, 2 * LANES), 2 * LANES)
            ids = [[inv_s[(r * NBLK + 2 * cb + e) // LANES, 0, lax.rem(r * NBLK + 2 * cb + e, LANES)]
                    for e in range(2)] for r in range(NBLK)]
            total = None if first else acc[:, at]
            for c in cs:
                rows = []
                for r in range(NBLK):
                    for e in range(2):
                        rows.append(jnp.concatenate(
                            [mbuf[ids[r][n], pl.ds(e * (span // 2) + STARTS[c], WIDTHS[c]), :] for n in range(2)],
                            axis=1))
                value = jnp.dot(lhs[c][...], jnp.concatenate(rows, axis=0), preferred_element_type=jnp.float32)
                total = value if total is None else total + value
            if last:
                out[:, at] = total.astype(jnp.bfloat16)
            else:
                acc[:, at] = total
            return carry
        lax.fori_loop(0, NBLK // 2, columns, 0, unroll=2)

    pl.semaphore_wait(barrier, 7)
    gather_start(0)
    wave_out(0)
    load_tiles.wait()
    tiles_out(0)
    for copy in load_own:
        copy.start()
    load_amp.start()

    def skip():
        pass

    def both(*events):
        def run():
            for event, *rest in events:
                event(*rest)
        return run

    for k in range(3):
        wave_next(k)
    gather_round(0, 0)
    wave_next(3)
    gather_round(0, 1)
    tiles_x(0)
    tiles_z(1)
    wave_next(4)
    gather_round(0, 2)
    gather_round(0, 3)
    gather_start(1)
    tiles_z(2)
    tiles_far(0)
    gather_far(0, 0)
    tiles_x(1)
    gather_far(0, 1)
    tiles_x(5)
    tiles_z(3)
    gather_done(0)
    load_amp.wait()
    contract_part(0, 0, [skip, both((gather_round, 1, 0)), skip, both((tiles_x, 2))])
    contract_part(0, 1, [both((gather_round, 1, 1)), both((tiles_z, 4)), both((tiles_x, 6)), skip])
    contract_part(0, 2, [both((tiles_far, 5)), both((tiles_far, 1)), both((gather_round, 1, 2)), skip])
    tiles_x(3)
    gather_round(1, 3)
    tiles_x(7)
    tiles_far(2)
    tiles_far(6)
    gather_far(1, 0)
    tiles_x(4)
    tiles_far(7)
    gather_far(1, 1)
    gather_done(1)
    contract_part(1, 0, [both((tiles_far, 3)), both((tiles_far, 4))])
    contract_part(1, 1)
    contract_part(1, 2)
    tiles_done()
    look_up()
    for u in range(SUBS):
        arrange(0, u)
    product((0,), True, False)
    for u in range(SUBS):
        arrange(1, u)
    product((1,), False, True)

    for c in range(CHUNKS):
        sent(fbuf[c].at[pl.ds(0, 3 * own)], ysend.at[c], yp.at[c, 0])
        sent(fbuf[c].at[pl.ds(0, NY * own)], ssend.at[c], sib.at[c])
        for u in range(SUBS):
            sent(sbuf[c].at[u, pl.ds(0, NAUX - 1)], asend.at[c, u], arecv.at[c, u])
    sent(mbuf.at[pl.ds(0, (NZ - 1) * half)], msend.at[0], msib.at[0])
    sent(mbuf.at[pl.ds(0, NZ * half)], msend.at[1], msib.at[0])
    sent(mbuf.at[pl.ds(0, NZ * half)], msend.at[2], msib.at[0])
    sent(mbuf.at[pl.ds(0, (NAUX - 1) * half)], msend.at[3], msib.at[0])
    sent(mbuf.at[pl.ds(0, NZ * half)], msend.at[4], msib.at[0])


def shards(factors, amplitudes, partners, metric_tiles, tile_pos):
    own, domain, aux_part = factors.shape
    nt, span = metric_tiles.shape[0], metric_tiles.shape[1]
    norb = own * 2 * NY
    rows = own * domain // NAUX
    dma = pltpu.SemaphoreType.DMA
    anywhere = pl.BlockSpec(memory_space=pl.ANY)
    scalars = pl.BlockSpec(memory_space=pltpu.SMEM)
    parts = [pltpu.VMEM((SUBS, NAUX, rows * pw // LANES // SUBS, LANES), jnp.bfloat16) for pw in WIDTHS]
    result = pl.pallas_call(
        kernel,
        out_shape=jax.ShapeDtypeStruct((rows, aux_part * NAUX), jnp.bfloat16),
        in_specs=[anywhere, anywhere, scalars, anywhere, scalars],
        out_specs=pl.BlockSpec(memory_space=pltpu.VMEM),
        scratch_shapes=[pltpu.VMEM((norb, pw, domain), jnp.bfloat16) for pw in WIDTHS] + parts + parts + [
            pltpu.VMEM((rows, pw * NAUX), jnp.bfloat16) for pw in WIDTHS] + [
            pltpu.VMEM(amplitudes.shape, jnp.bfloat16),
            pltpu.VMEM((NAUX * nt + 1, span + 16, span), jnp.bfloat16),
            pltpu.VMEM((NAUX, 16, LANES), jnp.float32),
            pltpu.VMEM((rows, aux_part * NAUX), jnp.float32),
            pltpu.VMEM((2, 8, LANES), jnp.int32),
            pltpu.SMEM((2, 8, LANES), jnp.int32),
            dma((3 + CHUNKS,)),
            dma((CHUNKS,)),
            dma((CHUNKS,)),
            dma((CHUNKS, max(PIECES))),
            dma((CHUNKS, max(PIECES))),
            dma((CHUNKS, max(PIECES) // 2)),
            dma((CHUNKS, max(PIECES) // 2)),
            dma((CHUNKS,)),
            dma((5,)),
            dma((NZ // 2,)),
            dma((NZ // 2,)),
            dma((NZ,)),
            dma((NZ,)),
            dma((NZ,)),
            dma((1,)),
            dma((CHUNKS, SUBS)),
            dma((CHUNKS, SUBS)),
            pltpu.SemaphoreType.REGULAR((WAVES + 2,)),
        ],
        compiler_params=pltpu.CompilerParams(
            collective_id=0, has_side_effects=True, vmem_limit_bytes=60 * 1024 * 1024),
    )(jnp.swapaxes(factors, 1, 2), amplitudes, partners.T, metric_tiles, tile_pos.T)
    return result.reshape(own, rows // own, aux_part * NAUX)


def solution(mesh):
    in_specs = (
        P("orb", None, "aux"),
        P("orb", None, None, None),
        P("orb", None),
        P("aux", None, None),
        P("aux", None),
    )
    out_specs = P("orb", "aux", None)
    return jax.shard_map(shards, mesh=mesh, in_specs=in_specs, out_specs=out_specs, check_vma=False)
```

time: 73.9 us -> 68.3 us (0.924)
  Pallas kernels: 69.9 us -> 65.7 us
  other arithmetic: 0.76 us -> 0 us
    pallas_call x1, Pallas kernels: 69.9 us -> 65.7 us  [shards(): pl.pallas_call(kernel, out_shape=jax.ShapeDtypeStruct((rows, aux_part * N...]
    convert_element_type x1 -> x0, other arithmetic: 0.76 us -> none  [shards(): keys = (tile_pos[:, 0] * NBLK + tile_pos[:, 1]).astype(jnp.bfloat16)]
where the time goes in v2:
time: 68.3 us; the launch traced here: 68.1 us
  Pallas kernels  65.7 us (96%)
  local copies, waits for them, and re-layouts  2.38 us (3%)
    pallas_call x1, Pallas kernels, shards(): pl.pallas_call(kernel, out_shape=jax.ShapeDtypeStruct((rows, aux_part * N...  65.7 us
    reshape x1, local copies, waits for them, and re-layouts, shards(): return result.reshape(own, rows // own, aux_part * NAUX)  2.38 us

profile of v2, /device:TPU:1, one launch (start us, length us, event | category | flops | bytes accessed | tf_op | source)
XLA Modules:
  0.0 68.1 jit_solution(13748175859875858600)
XLA Ops:
  0.0 65.7 %shard_map.55 = bf16[192,2048]{1,0:T(8,128)(2,1)} custom-call(bf16[48,64,128]{2,1,0:T(8,128)(2,1)} %bitcast.3, bf16[48,12,128,128]{3,2,1,0:T(8,128)(2,1)} %amp.1, s32[12,48]{1,0:T(8,128)} %bitcast.4, bf16[4,128,128]{2,1,0:T(8,128)(2,1)} %tiles.1, s32[2,4]{1,0:T(2,128)} %bitcast.5), custom_call_target="tpu_custom_call" | custom-call | tf_op jit(solution)/shard_map/pallas_call | solution.py:358
  65.7 2.4 %reshape.3 = bf16[48,4,2048]{2,1,0:T(4,128)(2,1)} reshape(bf16[192,2048]{1,0:T(8,128)(2,1)} %shard_map.55) | data formatting | bytes 1572864 | tf_op jit(solution)/shard_map/reshape | solution.py:393

commit v3 on v2

--- a/solution.py
+++ b/solution.py
@@ -20,11 +20,11 @@
 XMINUS = (5, 6, 7, 3)
 
 
-def kernel(ft, amp, part, tiles, pos, out, *scratch):
+def kernel(ft, amp, part_in, tiles, pos_in, result, *scratch):
     fbuf, sbuf, rbuf, lhs = (scratch[n * CHUNKS:(n + 1) * CHUNKS] for n in range(4))
-    (ampv, mbuf, stage, acc, inv_v, inv_s) = scratch[4 * CHUNKS:4 * CHUNKS + 6]
+    (ampv, mbuf, stage, acc, inv_v, inv_s, out, part, pos) = scratch[4 * CHUNKS:4 * CHUNKS + 9]
     (loc, ysend, ssend, yp, ym, y2p, y2m, sib,
-     msend, rzp, rzm, rxp, rxm, rx2, msib, asend, arecv, wave) = scratch[4 * CHUNKS + 6:]
+     msend, rz, rxp, rxm, rx2, msib, asend, arecv, wave) = scratch[4 * CHUNKS + 9:]
 
     o = lax.axis_index("orb")
     s = lax.axis_index("aux")
@@ -68,6 +68,11 @@
     mine = pl.ds(s * nt, nt)
     load_tiles = pltpu.make_async_copy(tiles, mbuf.at[mine, pl.ds(0, span)], loc.at[0])
     load_tiles.start()
+    load_pos = pltpu.make_async_copy(pos_in, pos, loc.at[3 + CHUNKS])
+    load_pos.start()
+    load_part = pltpu.make_async_copy(part_in, part, loc.at[4 + CHUNKS])
+    load_part.start()
+    load_pos.wait()
     for t in range(nt):
         key = (pos[0, t] * NBLK + pos[1, t]).astype(jnp.float32)
         mbuf[s * nt + t, pl.ds(span, 16), :] = jnp.full((16, LANES), key, jnp.float32).astype(jnp.bfloat16)
@@ -88,25 +93,29 @@
 
     def gather_start(c):
         npc = own // PIECES[c]
+        mid = PIECES[c] // 2
+
+        def put(q, ssem, rsem, dev):
+            src = ft.at[pl.ds(q * npc, npc), pl.ds(STARTS[c], WIDTHS[c]), :]
+            remote(src, fpiece(c, o, q), ssem, rsem, dev).start()
         for q in range(PIECES[c]):
-            src = ft.at[pl.ds(q * npc, npc), pl.ds(STARTS[c], WIDTHS[c]), :]
-            dst = fpiece(c, o, q)
-            remote(src, dst, ysend.at[c], yp.at[c, q], yplus).start()
-            remote(src, dst, ysend.at[c], ym.at[c, q], yminus).start()
+            below = (q + mid) % PIECES[c]
+            put(q, ysend.at[c], yp.at[c, q], yplus)
+            put(below, ysend.at[c], ym.at[c, below], yminus)
         for q in range(PIECES[c]):
-            src = ft.at[pl.ds(q * npc, npc), pl.ds(STARTS[c], WIDTHS[c]), :]
-            remote(src, fpiece(c, o, q), ssend.at[c], sib.at[c], sibling).start()
+            put(q, ssend.at[c], sib.at[c], sibling)
 
     def gather_round(c, q):
-        below, above = fpiece(c, orb_at(-1), q), fpiece(c, orb_at(1), q)
         mid = PIECES[c] // 2
+        high = (q + mid) % PIECES[c]
+        below, above = fpiece(c, orb_at(-1), q), fpiece(c, orb_at(1), high)
         recv(below, ysend.at[c], yp.at[c, q])
         if q < mid:
             remote(below, below, ysend.at[c], y2p.at[c, q], yplus).start()
         to_sibling(c, below)
-        recv(above, ysend.at[c], ym.at[c, q])
-        if q >= mid:
-            remote(above, above, ysend.at[c], y2m.at[c, q - mid], yminus).start()
+        recv(above, ysend.at[c], ym.at[c, high])
+        if q < mid:
+            remote(above, above, ysend.at[c], y2m.at[c, q], yminus).start()
         to_sibling(c, above)
 
     def gather_far(c, q):
@@ -125,18 +134,23 @@
         dz = -idx if idx <= NZ // 2 else idx - NZ // 2
         return mbuf.at[pl.ds(aux_at(dx, dz) * nt + h * half, half)]
 
-    def tiles_out(idx):
+    def tiles_x_out(idx):
         ref = shard(0, idx)
-        if idx < NZ // 2:
-            remote(ref, ref, msend.at[0], rzp.at[idx], zplus).start()
-        if idx == 0:
-            remote(ref, ref, msend.at[0], rzm.at[0], zminus).start()
-        elif idx > NZ // 2 and idx < NZ - 1:
-            remote(ref, ref, msend.at[0], rzm.at[idx - NZ // 2], zminus).start()
         remote(ref, ref, msend.at[1], rxp.at[idx], xplus).start()
         remote(ref, ref, msend.at[2], rxm.at[idx], xminus).start()
-        if idx:
-            remote(ref, ref, msend.at[3], msib.at[0], sibling).start()
+
+    def tiles_z_out():
+        ref = shard(0, 0)
+        for k in range(1, NZ // 2 + 1):
+            remote(ref, ref, msend.at[0], rz.at[k], (o, aux_at(0, k))).start()
+            if k < NZ // 2:
+                remote(ref, ref, msend.at[0], rz.at[NZ // 2 + k], (o, aux_at(0, -k))).start()
+
+    def tiles_z(idx):
+        ref = shard(0, idx)
+        recv(ref, msend.at[0], rz.at[idx])
+        tiles_x_out(idx)
+        remote(ref, ref, msend.at[3], msib.at[0], sibling).start()
 
     def tiles_x(idx):
         left, right = shard(-1, idx), shard(1, idx)
@@ -148,13 +162,6 @@
         if idx in XMINUS:
             remote(right, right, msend.at[4], rx2.at[idx], xminus).start()
         remote(right, right, msend.at[3], msib.at[0], sibling).start()
-
-    def tiles_z(k):
-        recv(shard(0, k), msend.at[0], rzp.at[k - 1])
-        tiles_out(k)
-        if k < NZ // 2:
-            recv(shard(0, NZ // 2 + k), msend.at[0], rzm.at[k - 1])
-            tiles_out(NZ // 2 + k)
 
     def tiles_far(idx):
         far = shard(2, idx)
@@ -266,6 +273,7 @@
                 total = value if total is None else total + value
             if last:
                 out[:, at] = total.astype(jnp.bfloat16)
+                pltpu.make_async_copy(out.at[:, at], result.at[:, at], loc.at[5 + CHUNKS]).start()
             else:
                 acc[:, at] = total
             return carry
@@ -275,7 +283,7 @@
     gather_start(0)
     wave_out(0)
     load_tiles.wait()
-    tiles_out(0)
+    tiles_x_out(0)
     for copy in load_own:
         copy.start()
     load_amp.start()
@@ -289,40 +297,43 @@
                 event(*rest)
         return run
 
-    for k in range(3):
+    for k in range(WAVES):
         wave_next(k)
+    tiles_z_out()
+    wave_next(3)
     gather_round(0, 0)
-    wave_next(3)
+    wave_next(4)
     gather_round(0, 1)
+    gather_start(1)
     tiles_x(0)
     tiles_z(1)
-    wave_next(4)
+    tiles_z(5)
+    tiles_far(0)
+    tiles_z(2)
     gather_round(0, 2)
+    tiles_z(6)
+    tiles_x(1)
+    tiles_x(5)
     gather_round(0, 3)
-    gather_start(1)
-    tiles_z(2)
-    tiles_far(0)
+    tiles_z(3)
+    tiles_z(7)
     gather_far(0, 0)
-    tiles_x(1)
+    tiles_x(2)
+    tiles_z(4)
     gather_far(0, 1)
-    tiles_x(5)
-    tiles_z(3)
     gather_done(0)
     load_amp.wait()
-    contract_part(0, 0, [skip, both((gather_round, 1, 0)), skip, both((tiles_x, 2))])
-    contract_part(0, 1, [both((gather_round, 1, 1)), both((tiles_z, 4)), both((tiles_x, 6)), skip])
-    contract_part(0, 2, [both((tiles_far, 5)), both((tiles_far, 1)), both((gather_round, 1, 2)), skip])
-    tiles_x(3)
+    load_part.wait()
+    contract_part(0, 0, [skip, both((gather_round, 1, 0)), both((tiles_x, 6)), both((tiles_far, 5), (tiles_far, 1))])
+    contract_part(0, 1, [both((gather_round, 1, 1)), both((tiles_x, 3)), both((tiles_x, 7)), skip])
+    contract_part(0, 2, [both((tiles_far, 6)), both((tiles_far, 2)), skip, both((gather_round, 1, 2))])
     gather_round(1, 3)
-    tiles_x(7)
-    tiles_far(2)
-    tiles_far(6)
-    gather_far(1, 0)
     tiles_x(4)
     tiles_far(7)
+    gather_far(1, 0)
     gather_far(1, 1)
     gather_done(1)
-    contract_part(1, 0, [both((tiles_far, 3)), both((tiles_far, 4))])
+    contract_part(1, 0, [skip, skip, skip, both((tiles_far, 3), (tiles_far, 4))])
     contract_part(1, 1)
     contract_part(1, 2)
     tiles_done()
@@ -334,6 +345,7 @@
         arrange(1, u)
     product((1,), False, True)
 
+    pltpu.make_async_copy(out, result, loc.at[5 + CHUNKS]).wait()
     for c in range(CHUNKS):
         sent(fbuf[c].at[pl.ds(0, 3 * own)], ysend.at[c], yp.at[c, 0])
         sent(fbuf[c].at[pl.ds(0, NY * own)], ssend.at[c], sib.at[c])
@@ -353,13 +365,12 @@
     rows = own * domain // NAUX
     dma = pltpu.SemaphoreType.DMA
     anywhere = pl.BlockSpec(memory_space=pl.ANY)
-    scalars = pl.BlockSpec(memory_space=pltpu.SMEM)
     parts = [pltpu.VMEM((SUBS, NAUX, rows * pw // LANES // SUBS, LANES), jnp.bfloat16) for pw in WIDTHS]
     result = pl.pallas_call(
         kernel,
         out_shape=jax.ShapeDtypeStruct((rows, aux_part * NAUX), jnp.bfloat16),
-        in_specs=[anywhere, anywhere, scalars, anywhere, scalars],
-        out_specs=pl.BlockSpec(memory_space=pltpu.VMEM),
+        in_specs=[anywhere] * 5,
+        out_specs=anywhere,
         scratch_shapes=[pltpu.VMEM((norb, pw, domain), jnp.bfloat16) for pw in WIDTHS] + parts + parts + [
             pltpu.VMEM((rows, pw * NAUX), jnp.bfloat16) for pw in WIDTHS] + [
             pltpu.VMEM(amplitudes.shape, jnp.bfloat16),
@@ -368,7 +379,10 @@
             pltpu.VMEM((rows, aux_part * NAUX), jnp.float32),
             pltpu.VMEM((2, 8, LANES), jnp.int32),
             pltpu.SMEM((2, 8, LANES), jnp.int32),
-            dma((3 + CHUNKS,)),
+            pltpu.VMEM((rows, aux_part * NAUX), jnp.bfloat16),
+            pltpu.SMEM(partners.shape[::-1], jnp.int32),
+            pltpu.SMEM(tile_pos.shape[::-1], jnp.int32),
+            dma((6 + CHUNKS,)),
             dma((CHUNKS,)),
             dma((CHUNKS,)),
             dma((CHUNKS, max(PIECES))),
@@ -377,8 +391,7 @@
             dma((CHUNKS, max(PIECES) // 2)),
             dma((CHUNKS,)),
             dma((5,)),
-            dma((NZ // 2,)),
-            dma((NZ // 2,)),
+            dma((NZ,)),
             dma((NZ,)),
             dma((NZ,)),
             dma((NZ,)),

time: 68.3 us -> 64.2 us (0.940)
  Pallas kernels: 65.7 us -> 61.7 us
    pallas_call x1, Pallas kernels: 65.7 us -> 61.7 us  [shards(): pl.pallas_call(kernel, out_shape=jax.ShapeDtypeStruct((rows, aux_part * N...]
where the time goes in v3:
time: 64.2 us; the launch traced here: 64.1 us
  Pallas kernels  61.7 us (96%)
  local copies, waits for them, and re-layouts  2.38 us (4%)
    pallas_call x1, Pallas kernels, shards(): pl.pallas_call(kernel, out_shape=jax.ShapeDtypeStruct((rows, aux_part * N...  61.7 us
    reshape x1, local copies, waits for them, and re-layouts, shards(): return result.reshape(own, rows // own, aux_part * NAUX)  2.38 us

profile of v3, /device:TPU:1, one launch (start us, length us, event | category | flops | bytes accessed | tf_op | source)
XLA Modules:
  0.0 64.1 jit_solution(11911320935596134124)
XLA Ops:
  0.0 61.7 %shard_map.55 = bf16[192,2048]{1,0:T(8,128)(2,1)} custom-call(bf16[48,64,128]{2,1,0:T(8,128)(2,1)} %bitcast.3, bf16[48,12,128,128]{3,2,1,0:T(8,128)(2,1)} %amp.1, s32[12,48]{1,0:T(8,128)} %bitcast.4, bf16[4,128,128]{2,1,0:T(8,128)(2,1)} %tiles.1, s32[2,4]{1,0:T(2,128)} %bitcast.5), custom_call_target="tpu_custom_call" | custom-call | tf_op jit(solution)/shard_map/pallas_call | solution.py:369
  61.7 2.4 %reshape.3 = bf16[48,4,2048]{2,1,0:T(4,128)(2,1)} reshape(bf16[192,2048]{1,0:T(8,128)(2,1)} %shard_map.55) | data formatting | bytes 1572864 | tf_op jit(solution)/shard_map/reshape | solution.py:406

commit v4 on v3

--- a/solution.py
+++ b/solution.py
@@ -324,17 +324,18 @@
     gather_done(0)
     load_amp.wait()
     load_part.wait()
-    contract_part(0, 0, [skip, both((gather_round, 1, 0)), both((tiles_x, 6)), both((tiles_far, 5), (tiles_far, 1))])
-    contract_part(0, 1, [both((gather_round, 1, 1)), both((tiles_x, 3)), both((tiles_x, 7)), skip])
-    contract_part(0, 2, [both((tiles_far, 6)), both((tiles_far, 2)), skip, both((gather_round, 1, 2))])
+    contract_part(0, 0, [skip, both((gather_round, 1, 0)), skip, both((gather_round, 1, 1))])
+    contract_part(0, 1, [both((tiles_x, 6)), both((tiles_far, 5), (tiles_far, 1)), skip, skip])
+    contract_part(0, 2, [both((tiles_x, 3)), both((gather_round, 1, 2)), skip, skip])
     gather_round(1, 3)
-    tiles_x(4)
-    tiles_far(7)
+    tiles_x(7)
+    tiles_far(6)
+    tiles_far(2)
     gather_far(1, 0)
     gather_far(1, 1)
     gather_done(1)
-    contract_part(1, 0, [skip, skip, skip, both((tiles_far, 3), (tiles_far, 4))])
-    contract_part(1, 1)
+    contract_part(1, 0, [skip, skip, skip, both((tiles_x, 4), (tiles_far, 7))])
+    contract_part(1, 1, [skip, skip, skip, both((tiles_far, 3), (tiles_far, 4))])
     contract_part(1, 2)
     tiles_done()
     look_up()

time: 64.2 us -> 62.5 us (0.974)
  Pallas kernels: 61.7 us -> 59.6 us
    pallas_call x1, Pallas kernels: 61.7 us -> 59.6 us  [shards(): pl.pallas_call(kernel, out_shape=jax.ShapeDtypeStruct((rows, aux_part * N...]
where the time goes in v4:
time: 62.5 us; the launch traced here: 62 us
  Pallas kernels  59.6 us (95%)
  local copies, waits for them, and re-layouts  2.38 us (4%)
    pallas_call x1, Pallas kernels, shards(): pl.pallas_call(kernel, out_shape=jax.ShapeDtypeStruct((rows, aux_part * N...  59.6 us
    reshape x1, local copies, waits for them, and re-layouts, shards(): return result.reshape(own, rows // own, aux_part * NAUX)  2.38 us

profile of v4, /device:TPU:1, one launch (start us, length us, event | category | flops | bytes accessed | tf_op | source)
XLA Modules:
  0.0 62.0 jit_solution(11879285306091457620)
XLA Ops:
  0.0 59.6 %shard_map.55 = bf16[192,2048]{1,0:T(8,128)(2,1)} custom-call(bf16[48,64,128]{2,1,0:T(8,128)(2,1)} %bitcast.3, bf16[48,12,128,128]{3,2,1,0:T(8,128)(2,1)} %amp.1, s32[12,48]{1,0:T(8,128)} %bitcast.4, bf16[4,128,128]{2,1,0:T(8,128)(2,1)} %tiles.1, s32[2,4]{1,0:T(2,128)} %bitcast.5), custom_call_target="tpu_custom_call" | custom-call | tf_op jit(solution)/shard_map/pallas_call | solution.py:370
  59.6 2.4 %reshape.3 = bf16[48,4,2048]{2,1,0:T(4,128)(2,1)} reshape(bf16[192,2048]{1,0:T(8,128)(2,1)} %shard_map.55) | data formatting | bytes 1572864 | tf_op jit(solution)/shard_map/reshape | solution.py:407
